TPU v7x, 32 devices: a whole 2x2x4 slice. The times are simulated.
32 devices in a mesh: mem: 8 (over y, x, core), st: 4 (over z).
Axes of the slice: x: 2, y: 2, z: 4, core: 2. Of those that a mesh axis runs over, the one named last changes fastest.
Arguments:
- ensemble: float32 [8192, 256], P('st', 'mem'), may hold values from -8 to 8
- obs_values: float32 [4, 8, 128], replicated, may hold values from -8 to 8
- obs_sigma: float32 [4, 8, 128], replicated, may hold values from 0.25 to 0.5
- obs_operator: float32 [4, 8, 2, 128, 128], replicated, may hold values from -0.375 to 0.375
- block_cols: int32 [4, 8, 2], replicated, may hold values from 0 to 63
- batch_order: int32 [4], replicated, may hold values from 0 to 3, each once
Outputs:
- analysis: float32 [8192, 256], P('st', 'mem')
- log_weights: float32 [256], P('mem')
- ess: float32 [], replicated
Inputs may be any that keep to these rules, and one draw needn't show every extreme that they name: `block_cols`: block indices of the whole state. `batch_order`: each batch exactly once.
All inputs are finite; a program needn't handle non-finite values.
Results may differ from a plain program's by a relative error of at most 0.0003.
Values sent between devices are 32-bit elements; how exact they have to be, the bound alone decides.
A program may use at most 64 MiB of HBM per device.

v0:
```python
import math
import jax
import jax.numpy as jnp
from jax import lax
from jax.sharding import PartitionSpec as P

precise = lax.Precision.HIGHEST


def solve_blocks(moment, target):
    factor = jnp.linalg.cholesky(moment)
    return jax.vmap(lambda lower, right: jax.scipy.linalg.cho_solve((lower, True), right))(
        factor, target
    )


def shards(ensemble, obs_values, obs_sigma, obs_operator, block_cols, batch_order):
    block_size = obs_operator.shape[-1]
    row_count, mem_dev = ensemble.shape
    nblocks = row_count // block_size
    members = mem_dev * lax.axis_size("mem")
    batches, obs_blocks, col_count = block_cols.shape
    temper = 1.0 / math.sqrt(batches * obs_blocks * block_size)
    offset = lax.axis_index("st") * nblocks
    states = ensemble.reshape(nblocks, block_size, mem_dev)
    eye = jnp.eye(block_size, dtype=jnp.float32)
    slots = jnp.arange(nblocks, dtype=jnp.int32)
    loglik = jnp.zeros((mem_dev,), jnp.float32)
    for batch_step in range(batches):
        chosen = batch_order[batch_step]
        operator_now = lax.dynamic_index_in_dim(obs_operator, chosen, 0, keepdims=False)
        columns = lax.dynamic_index_in_dim(block_cols, chosen, 0, keepdims=False)
        values_now = lax.dynamic_index_in_dim(obs_values, chosen, 0, keepdims=False)
        sigma_now = lax.dynamic_index_in_dim(obs_sigma, chosen, 0, keepdims=False)
        local_ids = columns.reshape(-1) - offset
        selector = (local_ids[:, None] == slots[None, :]).astype(jnp.float32)
        picked = jnp.einsum("ps,sim->pim", selector, states, precision=precise)
        picked = picked.reshape(obs_blocks, col_count, block_size, mem_dev)
        partial_value = jnp.einsum("bkij,bkjm->bim", operator_now, picked, precision=precise)
        image = lax.psum(partial_value, "st")
        misfit = (values_now[:, :, None] - image) / sigma_now[:, :, None]
        loglik = loglik - 0.5 * temper * jnp.sum(misfit * misfit, axis=(0, 1))
        center = lax.psum(jnp.sum(image, axis=2), "mem") / members
        anomaly = image - center[:, :, None]
        moment_sum, cross_sum = lax.psum(
            (
                jnp.einsum("bim,bjm->bij", anomaly, anomaly, precision=precise),
                jnp.einsum("bkim,bjm->bkij", picked, anomaly, precision=precise),
            ),
            "mem",
        )
        moment = moment_sum / (members - 1) + eye * (sigma_now * sigma_now)[:, :, None]
        cross = cross_sum / (members - 1)
        target = (values_now - center)[:, :, None] - 0.5 * anomaly
        weights = solve_blocks(moment, target)
        change = jnp.einsum("bkij,bjm->bkim", cross, weights, precision=precise)
        change = change.reshape(obs_blocks * col_count, block_size, mem_dev)
        states = states + jnp.einsum("ps,pim->sim", selector, change, precision=precise)
    largest_local = jnp.max(loglik)
    largest = lax.pmax(largest_local, "mem")
    scaled = jnp.exp(loglik - largest)
    summed, squares = lax.psum((jnp.sum(scaled), jnp.sum(scaled * scaled)), "mem")
    log_weights = loglik - largest - jnp.log(summed)
    ess = summed * summed / squares
    return (states.reshape(row_count, mem_dev), log_weights, ess)


def solution(mesh):
    placed = (P("st", "mem"), P(), P(), P(), P(), P())
    return jax.shard_map(
        shards,
        mesh=mesh,
        in_specs=placed,
        out_specs=(P("st", "mem"), P("mem"), P()),
        check_vma=False,
    )
```

profile of v0, /device:TPU:0, one launch (start us, length us, event | category | flops | bytes accessed | tf_op | source)
XLA Modules:
  0.0 1220.0 jit_solution(10032874839914542183)
XLA Ops:
  23.3 35.7 %all-reduce.14.cloned.1.call-done = f32[8,128,32]{1,2,0:T(8,128)} async-done(((f32[8,128,32]{1,2,0:T(8,128)}), f32[8,128,32]{1,2,0:T(8,128)}) %all-reduce.14.cloned.1.call-update) | async-done | bytes 131088 | tf_op jit(solution)/shard_map/psum | solution.py:40
  60.1 11.8 psum.127
  71.9 3.9 fusion.50
  79.3 57.4 %all-reduce.28.cloned.1.call-done = (f32[8,128,128]{1,2,0:T(8,128)}, f32[8,2,128,128]{3,2,1,0:T(8,128)}) async-done(((f32[8,128,128]{1,2,0:T(8,128)}, f32[8,2,128,128]{3,2,1,0:T(8,128)}), (f32[8,128,128]{1,2,0:T(8,128)}, f32[8,2,128,128]{3,2,1,0:T(8,128)})) %all-reduce.28.cloned.1.call-update) | async-done | bytes 1572880 | tf_op jit(solution)/shard_map/psum | solution.py:45
  139.2 93.8 %custom-call.14 = f32[8,128,128]{2,1,0:T(8,128)S(1)} custom-call(f32[8,128,128]{2,1,0:T(8,128)S(1)} %fusion.31), custom_call_target="Cholesky" | custom-call | tf_op jit(solution)/shard_map/jit(cholesky)/cholesky | solution.py:11
  233.3 78.6 %custom-call.15 = f32[8,1,128,128]{2,3,1,0:T(8,128)S(1)} custom-call(f32[8,1,128,128]{3,2,1,0:T(8,128)S(1)} %select_bitcast_fusion.3), custom_call_target="InvertDiagBlocksLowerTriangular" | custom-call | tf_op jit(solution)/shard_map/vmap(jit(_cho_solve))/triangular_solve | solution.py:12
  318.5 33.9 %all-reduce.16.cloned.1.call-done = f32[8,128,32]{1,2,0:T(8,128)} async-done(((f32[8,128,32]{1,2,0:T(8,128)}), f32[8,128,32]{1,2,0:T(8,128)}) %all-reduce.16.cloned.1.call-update) | async-done | bytes 131088 | tf_op jit(solution)/shard_map/psum | solution.py:40
  353.4 12.0 psum.131
  365.4 3.9 fusion.47
  372.4 57.8 %all-reduce.26.cloned.1.call-done = (f32[8,128,128]{1,2,0:T(8,128)}, f32[8,2,128,128]{3,2,1,0:T(8,128)}) async-done(((f32[8,128,128]{1,2,0:T(8,128)}, f32[8,2,128,128]{3,2,1,0:T(8,128)}), (f32[8,128,128]{1,2,0:T(8,128)}, f32[8,2,128,128]{3,2,1,0:T(8,128)})) %all-reduce.26.cloned.1.call-update) | async-done | bytes 1572880 | tf_op jit(solution)/shard_map/psum | solution.py:45
  432.8 93.8 %custom-call.16 = f32[8,128,128]{2,1,0:T(8,128)S(1)} custom-call(f32[8,128,128]{2,1,0:T(8,128)S(1)} %fusion.27), custom_call_target="Cholesky" | custom-call | tf_op jit(solution)/shard_map/jit(cholesky)/cholesky | solution.py:11
  526.9 78.6 %custom-call.17 = f32[8,1,128,128]{2,3,1,0:T(8,128)S(1)} custom-call(f32[8,1,128,128]{3,2,1,0:T(8,128)S(1)} %select_bitcast_fusion.2), custom_call_target="InvertDiagBlocksLowerTriangular" | custom-call | tf_op jit(solution)/shard_map/vmap(jit(_cho_solve))/triangular_solve | solution.py:12
  612.0 33.9 %all-reduce.18.cloned.1.call-done = f32[8,128,32]{1,2,0:T(8,128)} async-done(((f32[8,128,32]{1,2,0:T(8,128)}), f32[8,128,32]{1,2,0:T(8,128)}) %all-reduce.18.cloned.1.call-update) | async-done | bytes 131088 | tf_op jit(solution)/shard_map/psum | solution.py:40
  647.0 12.2 %psum.135 = f32[8,128]{1,0:T(8,128)S(1)} all-reduce(f32[8,128]{1,0:T(8,128)S(1)} %get-tuple-element.10), channel_id=1, replica_groups=mesh['mem'=8,'st'=4] {'mem'}, use_global_device_ids=true, to_apply=%region_14.17 | all-reduce | flops 1024 | bytes 8192 | tf_op jit(solution)/shard_map/psum | solution.py:43
  666.2 57.8 %all-reduce.24.cloned.1.call-done = (f32[8,128,128]{1,2,0:T(8,128)}, f32[8,2,128,128]{3,2,1,0:T(8,128)}) async-done(((f32[8,128,128]{1,2,0:T(8,128)}, f32[8,2,128,128]{3,2,1,0:T(8,128)}), (f32[8,128,128]{1,2,0:T(8,128)}, f32[8,2,128,128]{3,2,1,0:T(8,128)})) %all-reduce.24.cloned.1.call-update) | async-done | bytes 1572880 | tf_op jit(solution)/shard_map/psum | solution.py:45
  726.5 93.8 %custom-call.18 = f32[8,128,128]{2,1,0:T(8,128)S(1)} custom-call(f32[8,128,128]{2,1,0:T(8,128)S(1)} %fusion.23), custom_call_target="Cholesky" | custom-call | tf_op jit(solution)/shard_map/jit(cholesky)/cholesky | solution.py:11
  820.6 78.6 %custom-call.19 = f32[8,1,128,128]{2,3,1,0:T(8,128)S(1)} custom-call(f32[8,1,128,128]{3,2,1,0:T(8,128)S(1)} %select_bitcast_fusion.1), custom_call_target="InvertDiagBlocksLowerTriangular" | custom-call | tf_op jit(solution)/shard_map/vmap(jit(_cho_solve))/triangular_solve | solution.py:12
  905.8 33.9 %all-reduce.20.cloned.1.call-done = f32[8,128,32]{1,2,0:T(8,128)} async-done(((f32[8,128,32]{1,2,0:T(8,128)}), f32[8,128,32]{1,2,0:T(8,128)}) %all-reduce.20.cloned.1.call-update) | async-done | bytes 131088 | tf_op jit(solution)/shard_map/psum | solution.py:40
  941.3 12.4 %pmax.7 = f32[]{:T(128)} all-reduce(f32[]{:T(128)} %get-tuple-element.28), channel_id=1, replica_groups=mesh['mem'=8,'st'=4] {'mem'}, use_global_device_ids=true, to_apply=%region_27.30 | all-reduce | flops 1 | bytes 8 | tf_op jit(solution)/shard_map/pmax | solution.py:60
  955.0 12.8 %all-reduce = (f32[8,128]{1,0:T(8,128)S(1)}, f32[]{:T(128)}, f32[]{:T(128)}) all-reduce(f32[8,128]{1,0:T(8,128)S(1)} %get-tuple-element.12, f32[]{:T(128)} %get-tuple-element.14, f32[]{:T(128)} %get-tuple-element.13), channel_id=1, replica_groups=mesh['mem'=8,'st'=4] {'mem'}, use_global_device_ids=true, to_apply=%region_19.22 | all-reduce | flops 1026 | bytes 8208 | tf_op jit(solution)/shard_map/psum | solution.py:43
  967.8 3.9 fusion.41
  978.4 54.3 %all-reduce.22.cloned.1.call-done = (f32[8,128,128]{1,2,0:T(8,128)}, f32[8,2,128,128]{3,2,1,0:T(8,128)}) async-done(((f32[8,128,128]{1,2,0:T(8,128)}, f32[8,2,128,128]{3,2,1,0:T(8,128)}), (f32[8,128,128]{1,2,0:T(8,128)}, f32[8,2,128,128]{3,2,1,0:T(8,128)})) %all-reduce.22.cloned.1.call-update) | async-done | bytes 1572880 | tf_op jit(solution)/shard_map/psum | solution.py:45
  1035.2 93.8 %custom-call.20 = f32[8,128,128]{2,1,0:T(8,128)S(1)} custom-call(f32[8,128,128]{2,1,0:T(8,128)S(1)} %fusion.19), custom_call_target="Cholesky" | custom-call | tf_op jit(solution)/shard_map/jit(cholesky)/cholesky | solution.py:11
  1129.3 78.6 %custom-call.21 = f32[8,1,128,128]{2,3,1,0:T(8,128)S(1)} custom-call(f32[8,1,128,128]{3,2,1,0:T(8,128)S(1)} %select_bitcast_fusion), custom_call_target="InvertDiagBlocksLowerTriangular" | custom-call | tf_op jit(solution)/shard_map/vmap(jit(_cho_solve))/triangular_solve | solution.py:12
  (113 shorter events, 66.5 us)
Async XLA Ops:
  7.2 51.9 %all-reduce.14.cloned.1.call-start = ((), (), s32[]{:S(2)}) async-start(), calls=%async_computation | async-start | bytes 262144 | tf_op jit(solution)/shard_map/psum | solution.py:40
  21.8 114.9 %all-reduce.28.cloned.1.call-start = ((), (), s32[]{:S(2)}) async-start(), calls=%async_computation.7 | async-start | bytes 3145728 | tf_op jit(solution)/shard_map/psum | solution.py:45
  75.8 236.1 %copy-start.1 = (f32[8,128,32]{1,2,0:T(8,128)S(1)}, f32[8,128,32]{1,2,0:T(8,128)}, u32[]{:S(2)}) copy-start(f32[8,128,32]{1,2,0:T(8,128)} %all-reduce.14.cloned.1.call-done) | copy-start | bytes 393220
  78.7 273.7 %all-reduce.16.cloned.1.call-start = ((), (), s32[]{:S(2)}) async-start(), calls=%async_computation.1 | async-start | bytes 262144 | tf_op jit(solution)/shard_map/psum | solution.py:40
  136.7 176.7 %copy-start.5 = (f32[8,2,128,128]{3,2,1,0:T(8,128)S(1)}, f32[8,2,128,128]{3,2,1,0:T(8,128)}, u32[]{:S(2)}) copy-start(f32[8,2,128,128]{3,2,1,0:T(8,128)} %get-tuple-element.25) | copy-start | bytes 3145732
  318.5 111.8 %all-reduce.26.cloned.1.call-start = ((), (), s32[]{:S(2)}) async-start(), calls=%async_computation.6 | async-start | bytes 3145728 | tf_op jit(solution)/shard_map/psum | solution.py:45
  369.3 236.1 %copy-start.3 = (f32[8,128,32]{1,2,0:T(8,128)S(1)}, f32[8,128,32]{1,2,0:T(8,128)}, u32[]{:S(2)}) copy-start(f32[8,128,32]{1,2,0:T(8,128)} %all-reduce.16.cloned.1.call-done) | copy-start | bytes 393220
  372.2 273.7 %all-reduce.18.cloned.1.call-start = ((), (), s32[]{:S(2)}) async-start(), calls=%async_computation.2 | async-start | bytes 262144 | tf_op jit(solution)/shard_map/psum | solution.py:40
  430.2 176.7 %copy-start.7 = (f32[8,2,128,128]{3,2,1,0:T(8,128)S(1)}, f32[8,2,128,128]{3,2,1,0:T(8,128)}, u32[]{:S(2)}) copy-start(f32[8,2,128,128]{3,2,1,0:T(8,128)} %get-tuple-element.23) | copy-start | bytes 3145732
  612.0 112.0 %all-reduce.24.cloned.1.call-start = ((), (), s32[]{:S(2)}) async-start(), calls=%async_computation.5 | async-start | bytes 3145728 | tf_op jit(solution)/shard_map/psum | solution.py:45
  663.1 236.1 %copy-start.2 = (f32[8,128,32]{1,2,0:T(8,128)S(1)}, f32[8,128,32]{1,2,0:T(8,128)}, u32[]{:S(2)}) copy-start(f32[8,128,32]{1,2,0:T(8,128)} %all-reduce.18.cloned.1.call-done) | copy-start | bytes 393220
  666.0 273.7 %all-reduce.20.cloned.1.call-start = ((), (), s32[]{:S(2)}) async-start(), calls=%async_computation.3 | async-start | bytes 262144 | tf_op jit(solution)/shard_map/psum | solution.py:40
  724.0 176.7 %copy-start.6 = (f32[8,2,128,128]{3,2,1,0:T(8,128)S(1)}, f32[8,2,128,128]{3,2,1,0:T(8,128)}, u32[]{:S(2)}) copy-start(f32[8,2,128,128]{3,2,1,0:T(8,128)} %get-tuple-element.21) | copy-start | bytes 3145732
  905.7 127.0 %all-reduce.22.cloned.1.call-start = ((), (), s32[]{:S(2)}) async-start(), calls=%async_computation.4 | async-start | bytes 3145728 | tf_op jit(solution)/shard_map/psum | solution.py:45
  971.7 236.2 %copy-start = (f32[8,128,32]{1,2,0:T(8,128)S(1)}, f32[8,128,32]{1,2,0:T(8,128)}, u32[]{:S(2)}) copy-start(f32[8,128,32]{1,2,0:T(8,128)} %all-reduce.20.cloned.1.call-done) | copy-start | bytes 393220
  1032.7 176.7 %copy-start.4 = (f32[8,2,128,128]{3,2,1,0:T(8,128)S(1)}, f32[8,2,128,128]{3,2,1,0:T(8,128)}, u32[]{:S(2)}) copy-start(f32[8,2,128,128]{3,2,1,0:T(8,128)} %get-tuple-element.19) | copy-start | bytes 3145732
Sparse Core Ops, SparseCore 0:
  21.9 37.1 all-reduce.13
  78.8 57.8 all-reduce.27
  318.6 33.7 all-reduce.15
  372.3 57.8 all-reduce.25
  612.1 33.7 all-reduce.17
  666.1 57.8 all-reduce.23
  905.9 33.7 all-reduce.19
  974.7 57.9 all-reduce.21
where the time goes:
time: 1220 us
  other arithmetic  709 us (58%)
  waiting for transfers between devices  365 us (30%)
  blocking collectives  61.3 us (5%)
  matrix products  52.9 us (4%)
  between operations  26.4 us (2%)
    another operation x13, other arithmetic, solve_blocks(): factor = jnp.linalg.cholesky(moment)  376 us
    another operation x9, other arithmetic, solve_blocks(): jax.scipy.linalg.cho_solve((lower, True), right)  315 us
    psum x4, waiting for transfers between devices, shards(): lax.psum((jnp.einsum('bim,bjm->bij', anomaly, anomaly, precision=precise)...  227 us
    psum x4, waiting for transfers between devices, shards(): image = lax.psum(partial_value, 'st')  137 us
    psum x4, blocking collectives, shards(): center = lax.psum(jnp.sum(image, axis=2), 'mem') / members  48.9 us
  transfers between devices with their start and end apart: 8, of which 8 were waited for; matrix products, arithmetic and copies ran while one was open for 0% of the time, Pallas kernels for 0%

commit v1 on v0

--- a/solution.py
+++ b/solution.py
@@ -37,7 +37,7 @@
         picked = jnp.einsum("ps,sim->pim", selector, states, precision=precise)
         picked = picked.reshape(obs_blocks, col_count, block_size, mem_dev)
         partial_value = jnp.einsum("bkij,bkjm->bim", operator_now, picked, precision=precise)
-        image = lax.psum(partial_value, "st")
+        image = jnp.sum(lax.all_gather(partial_value, "st"), axis=0)
         misfit = (values_now[:, :, None] - image) / sigma_now[:, :, None]
         loglik = loglik - 0.5 * temper * jnp.sum(misfit * misfit, axis=(0, 1))
         center = lax.psum(jnp.sum(image, axis=2), "mem") / members

time: 1220 us -> 1140 us (0.934)
  waiting for transfers between devices: 365 us -> 231 us
  blocking collectives: 61.3 us -> 124 us
    psum x4 -> x0, waiting for transfers between devices: 137 us -> none  [shards(): image = lax.psum(partial_value, 'st')]
    all_gather x0 -> x4, blocking collectives: none -> 62.6 us  [shards(): image = jnp.sum(lax.all_gather(partial_value, 'st'), axis=0)]
  transfers between devices with their start and end apart: 8 -> 4, of which waited for: 8 -> 4; matrix products, arithmetic and copies ran while one was open for 0% -> 0% of each run, Pallas kernels for 0% -> 0%
where the time goes in v1:
time: 1140 us; the launch traced here: 1130 us
  other arithmetic  705 us (62%)
  waiting for transfers between devices  231 us (20%)
  blocking collectives  124 us (11%)
  matrix products  42.4 us (4%)
  between operations  26.1 us (2%)
    another operation x13, other arithmetic, solve_blocks(): factor = jnp.linalg.cholesky(moment)  376 us
    another operation x9, other arithmetic, solve_blocks(): jax.scipy.linalg.cho_solve((lower, True), right)  315 us
    psum x4, waiting for transfers between devices, shards(): lax.psum((jnp.einsum('bim,bjm->bij', anomaly, anomaly, precision=precise)...  231 us
    all_gather x4, blocking collectives, shards(): image = jnp.sum(lax.all_gather(partial_value, 'st'), axis=0)  62.6 us
    psum x4, blocking collectives, shards(): center = lax.psum(jnp.sum(image, axis=2), 'mem') / members  49.3 us
  transfers between devices with their start and end apart: 4, of which 4 were waited for; matrix products, arithmetic and copies ran while one was open for 0% of the time, Pallas kernels for 0%

profile of v1, /device:TPU:0, one launch (start us, length us, event | category | flops | bytes accessed | tf_op | source)
XLA Modules:
  0.0 1134.0 jit_solution(12855763376074155377)
XLA Ops:
  21.1 17.4 %all-gather = f32[32,128,32]{1,2,0:T(8,128)S(1)} all-gather(f32[8,128,32]{1,2,0:T(8,128)S(1)} %convolution_bitcast_fusion.7), channel_id=2, replica_groups=mesh['mem'=8,'st'=4] {'st'}, dimensions={0}, use_global_device_ids=true | all-gather | bytes 655360 | tf_op jit(solution)/shard_map/all_gather | solution.py:40
  38.6 12.2 %psum.98 = f32[8,128]{1,0:T(8,128)S(1)} all-reduce(f32[8,128]{1,0:T(8,128)S(1)} %bitcast_reduce_fusion.3), channel_id=1, replica_groups=mesh['mem'=8,'st'=4] {'mem'}, use_global_device_ids=true, to_apply=%region_2.3 | all-reduce | flops 1024 | bytes 8192 | tf_op jit(solution)/shard_map/psum | solution.py:43
  52.6 3.0 fusion.50
  56.3 59.0 %all-reduce.16.cloned.1.call-done = (f32[8,128,128]{1,2,0:T(8,128)}, f32[8,2,128,128]{3,2,1,0:T(8,128)}) async-done(((f32[8,128,128]{1,2,0:T(8,128)}, f32[8,2,128,128]{3,2,1,0:T(8,128)}), (f32[8,128,128]{1,2,0:T(8,128)}, f32[8,2,128,128]{3,2,1,0:T(8,128)})) %all-reduce.16.cloned.1.call-update) | async-done | bytes 1572880 | tf_op jit(solution)/shard_map/psum | solution.py:45
  117.9 93.8 %custom-call.14 = f32[8,128,128]{2,1,0:T(8,128)S(1)} custom-call(f32[8,128,128]{2,1,0:T(8,128)S(1)} %fusion.31), custom_call_target="Cholesky" | custom-call | tf_op jit(solution)/shard_map/jit(cholesky)/cholesky | solution.py:11
  212.0 78.6 %custom-call.15 = f32[8,1,128,128]{2,3,1,0:T(8,128)S(1)} custom-call(f32[8,1,128,128]{3,2,1,0:T(8,128)S(1)} %select_bitcast_fusion.3), custom_call_target="InvertDiagBlocksLowerTriangular" | custom-call | tf_op jit(solution)/shard_map/vmap(jit(_cho_solve))/triangular_solve | solution.py:12
  296.4 15.1 %all-gather.1 = f32[32,128,32]{1,2,0:T(8,128)S(1)} all-gather(f32[8,128,32]{1,2,0:T(8,128)S(1)} %convolution_bitcast_fusion.6), channel_id=3, replica_groups=mesh['mem'=8,'st'=4] {'st'}, dimensions={0}, use_global_device_ids=true | all-gather | bytes 655360 | tf_op jit(solution)/shard_map/all_gather | solution.py:40
  311.6 12.2 %psum.101 = f32[8,128]{1,0:T(8,128)S(1)} all-reduce(f32[8,128]{1,0:T(8,128)S(1)} %bitcast_reduce_fusion.2), channel_id=1, replica_groups=mesh['mem'=8,'st'=4] {'mem'}, use_global_device_ids=true, to_apply=%region_9.12 | all-reduce | flops 1024 | bytes 8192 | tf_op jit(solution)/shard_map/psum | solution.py:43
  325.6 3.0 fusion.47
  328.9 58.7 %all-reduce.14.cloned.1.call-done = (f32[8,128,128]{1,2,0:T(8,128)}, f32[8,2,128,128]{3,2,1,0:T(8,128)}) async-done(((f32[8,128,128]{1,2,0:T(8,128)}, f32[8,2,128,128]{3,2,1,0:T(8,128)}), (f32[8,128,128]{1,2,0:T(8,128)}, f32[8,2,128,128]{3,2,1,0:T(8,128)})) %all-reduce.14.cloned.1.call-update) | async-done | bytes 1572880 | tf_op jit(solution)/shard_map/psum | solution.py:45
  390.1 93.8 %custom-call.16 = f32[8,128,128]{2,1,0:T(8,128)S(1)} custom-call(f32[8,128,128]{2,1,0:T(8,128)S(1)} %fusion.27), custom_call_target="Cholesky" | custom-call | tf_op jit(solution)/shard_map/jit(cholesky)/cholesky | solution.py:11
  484.1 78.6 %custom-call.17 = f32[8,1,128,128]{2,3,1,0:T(8,128)S(1)} custom-call(f32[8,1,128,128]{3,2,1,0:T(8,128)S(1)} %select_bitcast_fusion.2), custom_call_target="InvertDiagBlocksLowerTriangular" | custom-call | tf_op jit(solution)/shard_map/vmap(jit(_cho_solve))/triangular_solve | solution.py:12
  568.6 15.1 %all-gather.2 = f32[32,128,32]{1,2,0:T(8,128)S(1)} all-gather(f32[8,128,32]{1,2,0:T(8,128)S(1)} %convolution_bitcast_fusion.5), channel_id=4, replica_groups=mesh['mem'=8,'st'=4] {'st'}, dimensions={0}, use_global_device_ids=true | all-gather | bytes 655360 | tf_op jit(solution)/shard_map/all_gather | solution.py:40
  583.8 12.0 %psum.104 = f32[8,128]{1,0:T(8,128)S(1)} all-reduce(f32[8,128]{1,0:T(8,128)S(1)} %bitcast_reduce_fusion.1), channel_id=1, replica_groups=mesh['mem'=8,'st'=4] {'mem'}, use_global_device_ids=true, to_apply=%region_14.17 | all-reduce | flops 1024 | bytes 8192 | tf_op jit(solution)/shard_map/psum | solution.py:43
  597.6 3.0 fusion.44
  601.2 58.4 %all-reduce.12.cloned.1.call-done = (f32[8,128,128]{1,2,0:T(8,128)}, f32[8,2,128,128]{3,2,1,0:T(8,128)}) async-done(((f32[8,128,128]{1,2,0:T(8,128)}, f32[8,2,128,128]{3,2,1,0:T(8,128)}), (f32[8,128,128]{1,2,0:T(8,128)}, f32[8,2,128,128]{3,2,1,0:T(8,128)})) %all-reduce.12.cloned.1.call-update) | async-done | bytes 1572880 | tf_op jit(solution)/shard_map/psum | solution.py:45
  662.1 93.8 %custom-call.18 = f32[8,128,128]{2,1,0:T(8,128)S(1)} custom-call(f32[8,128,128]{2,1,0:T(8,128)S(1)} %fusion.23), custom_call_target="Cholesky" | custom-call | tf_op jit(solution)/shard_map/jit(cholesky)/cholesky | solution.py:11
  756.2 78.6 %custom-call.19 = f32[8,1,128,128]{2,3,1,0:T(8,128)S(1)} custom-call(f32[8,1,128,128]{3,2,1,0:T(8,128)S(1)} %select_bitcast_fusion.1), custom_call_target="InvertDiagBlocksLowerTriangular" | custom-call | tf_op jit(solution)/shard_map/vmap(jit(_cho_solve))/triangular_solve | solution.py:12
  840.7 15.1 %all-gather.3 = f32[32,128,32]{1,2,0:T(8,128)S(1)} all-gather(f32[8,128,32]{1,2,0:T(8,128)S(1)} %convolution_bitcast_fusion.4), channel_id=5, replica_groups=mesh['mem'=8,'st'=4] {'st'}, dimensions={0}, use_global_device_ids=true | all-gather | bytes 655360 | tf_op jit(solution)/shard_map/all_gather | solution.py:40
  856.6 12.4 %pmax.7 = f32[]{:T(128)} all-reduce(f32[]{:T(128)} %get-tuple-element.20), channel_id=1, replica_groups=mesh['mem'=8,'st'=4] {'mem'}, use_global_device_ids=true, to_apply=%region_27.30 | all-reduce | flops 1 | bytes 8 | tf_op jit(solution)/shard_map/pmax | solution.py:60
  870.3 12.9 %all-reduce = (f32[8,128]{1,0:T(8,128)S(1)}, f32[]{:T(128)}, f32[]{:T(128)}) all-reduce(f32[8,128]{1,0:T(8,128)S(1)} %bitcast_reduce_fusion, f32[]{:T(128)} %get-tuple-element.6, f32[]{:T(128)} %get-tuple-element.5), channel_id=1, replica_groups=mesh['mem'=8,'st'=4] {'mem'}, use_global_device_ids=true, to_apply=%region_19.22 | all-reduce | flops 1026 | bytes 8208 | tf_op jit(solution)/shard_map/psum | solution.py:43
  891.9 55.1 %all-reduce.10.cloned.1.call-done = (f32[8,128,128]{1,2,0:T(8,128)}, f32[8,2,128,128]{3,2,1,0:T(8,128)}) async-done(((f32[8,128,128]{1,2,0:T(8,128)}, f32[8,2,128,128]{3,2,1,0:T(8,128)}), (f32[8,128,128]{1,2,0:T(8,128)}, f32[8,2,128,128]{3,2,1,0:T(8,128)})) %all-reduce.10.cloned.1.call-update) | async-done | bytes 1572880 | tf_op jit(solution)/shard_map/psum | solution.py:45
  949.5 93.8 %custom-call.20 = f32[8,128,128]{2,1,0:T(8,128)S(1)} custom-call(f32[8,128,128]{2,1,0:T(8,128)S(1)} %fusion.19), custom_call_target="Cholesky" | custom-call | tf_op jit(solution)/shard_map/jit(cholesky)/cholesky | solution.py:11
  1043.6 78.6 %custom-call.21 = f32[8,1,128,128]{2,3,1,0:T(8,128)S(1)} custom-call(f32[8,1,128,128]{3,2,1,0:T(8,128)S(1)} %select_bitcast_fusion), custom_call_target="InvertDiagBlocksLowerTriangular" | custom-call | tf_op jit(solution)/shard_map/vmap(jit(_cho_solve))/triangular_solve | solution.py:12
  (113 shorter events, 53.9 us)
Async XLA Ops:
  7.2 43.6 %copy-start.4 = (f32[4,8,128]{2,1,0:T(8,128)S(1)}, f32[4,8,128]{2,1,0:T(8,128)}, u32[]{:S(2)}) copy-start(f32[4,8,128]{2,1,0:T(8,128)} %param.10) | copy-start | bytes 49156
  7.2 49.1 %copy-start.5 = (f32[4,8,128]{2,1,0:T(8,128)S(1)}, f32[4,8,128]{2,1,0:T(8,128)}, u32[]{:S(2)}) copy-start(f32[4,8,128]{2,1,0:T(8,128)} %param.11) | copy-start | bytes 49156
  7.2 108.2 %all-reduce.16.cloned.1.call-start = ((), (), s32[]{:S(2)}) async-start(), calls=%async_computation.3 | async-start | bytes 3145728 | tf_op jit(solution)/shard_map/psum | solution.py:45
  55.7 331.9 %all-reduce.14.cloned.1.call-start = ((), (), s32[]{:S(2)}) async-start(), calls=%async_computation.2 | async-start | bytes 3145728 | tf_op jit(solution)/shard_map/psum | solution.py:45
  115.3 176.7 %copy-start = (f32[8,2,128,128]{3,2,1,0:T(8,128)S(1)}, f32[8,2,128,128]{3,2,1,0:T(8,128)}, u32[]{:S(2)}) copy-start(f32[8,2,128,128]{3,2,1,0:T(8,128)} %get-tuple-element.17) | copy-start | bytes 3145732
  328.6 331.0 %all-reduce.12.cloned.1.call-start = ((), (), s32[]{:S(2)}) async-start(), calls=%async_computation.1 | async-start | bytes 3145728 | tf_op jit(solution)/shard_map/psum | solution.py:45
  387.5 176.7 %copy-start.3 = (f32[8,2,128,128]{3,2,1,0:T(8,128)S(1)}, f32[8,2,128,128]{3,2,1,0:T(8,128)}, u32[]{:S(2)}) copy-start(f32[8,2,128,128]{3,2,1,0:T(8,128)} %get-tuple-element.15) | copy-start | bytes 3145732
  600.6 346.4 %all-reduce.10.cloned.1.call-start = ((), (), s32[]{:S(2)}) async-start(), calls=%async_computation | async-start | bytes 3145728 | tf_op jit(solution)/shard_map/psum | solution.py:45
  659.6 176.7 %copy-start.1 = (f32[8,2,128,128]{3,2,1,0:T(8,128)S(1)}, f32[8,2,128,128]{3,2,1,0:T(8,128)}, u32[]{:S(2)}) copy-start(f32[8,2,128,128]{3,2,1,0:T(8,128)} %get-tuple-element.13) | copy-start | bytes 3145732
  947.0 176.7 %copy-start.2 = (f32[8,2,128,128]{3,2,1,0:T(8,128)S(1)}, f32[8,2,128,128]{3,2,1,0:T(8,128)}, u32[]{:S(2)}) copy-start(f32[8,2,128,128]{3,2,1,0:T(8,128)} %get-tuple-element.11) | copy-start | bytes 3145732
Sparse Core Ops, SparseCore 0:
  55.8 59.5 all-reduce.15
  328.8 58.7 all-reduce.13
  600.7 58.8 all-reduce.11
  888.2 58.7 all-reduce.9
